TPU v7x, 32 devices: a whole 2x2x4 slice. The times are simulated.
32 devices in a mesh: ctx: 16 (over z, x, core), head: 2 (over y).
Axes of the slice: x: 2, y: 2, z: 4, core: 2. Of those that a mesh axis runs over, the one named last changes fastest.
Arguments:
- queries: bfloat16 [64, 2048], P(('ctx', 'head')), may hold values from -150 to 150
- new_block_keys: bfloat16 [64, 512], P(('ctx', 'head')), may hold values from -6 to 6
- new_block_values: bfloat16 [64, 512], P(('ctx', 'head')), may hold values from -6 to 6
- stored_keys: bfloat16 [7168, 512], P('ctx', 'head'), may hold values from -6 to 6
- stored_values: bfloat16 [7168, 512], P('ctx', 'head'), may hold values from -6 to 6
- stretch_start: int32 [1], replicated, may hold values from 3584 to 7168
- block_order: int32 [32], replicated, may hold values from 0 to 31, each once
Outputs:
- attended: bfloat16 [64, 2048], P(('ctx', 'head'))
Inputs may be any that keep to these rules, and one draw needn't show every extreme that they name: `block_order`: each value appears once.
All inputs are finite; a program needn't handle non-finite values.
Results may differ from a plain program's by a relative error of at most 0.0049.
Values may be sent and summed in bfloat16 or wider, within the bound.
A program may use at most 128 MiB of HBM per device.

v0:
```python
import math
import jax
import jax.numpy as jnp
from jax import lax
from jax.sharding import PartitionSpec as P

QUERY_HEADS = 16
KEY_VALUE_HEADS = 4
HEAD_WIDTH = 128
NEG_FILL = -1e30


def on_device(
    queries,
    new_block_keys,
    new_block_values,
    stored_keys,
    stored_values,
    stretch_start,
    block_order,
):
    local_query, local_keys, local_values = (
        lax.all_to_all(queries, "head", split_axis=1, concat_axis=0, tiled=True),
        lax.all_to_all(new_block_keys, "head", split_axis=1, concat_axis=0, tiled=True),
        lax.all_to_all(new_block_values, "head", split_axis=1, concat_axis=0, tiled=True),
    )
    query_rows = local_keys.shape[0]
    cache_rows = stored_keys.shape[0]
    kv_width = local_keys.shape[1]
    kv_heads = kv_width // HEAD_WIDTH
    query_group_width = QUERY_HEADS // KEY_VALUE_HEADS
    half_rows = query_rows // 2
    stretch_first = stretch_start[0]
    context = lax.axis_index("ctx")
    fresh_rows = context * query_rows + jnp.arange(query_rows, dtype=jnp.int32)
    fresh_pos = (
        stretch_first + block_order[fresh_rows // half_rows] * half_rows + fresh_rows % half_rows
    )
    cache_pos = context * cache_rows + jnp.arange(cache_rows, dtype=jnp.int32)
    key_pos = jnp.concatenate([fresh_pos, cache_pos])
    usable = jnp.concatenate([jnp.ones((query_rows,), dtype=bool), cache_pos < stretch_first])
    key_count = query_rows + cache_rows
    key_rows = jnp.concatenate([local_keys, stored_keys], axis=0).reshape(
        key_count, kv_heads, HEAD_WIDTH
    )
    value_rows = jnp.concatenate([local_values, stored_values], axis=0).reshape(
        key_count, kv_heads, HEAD_WIDTH
    )
    score_scale = 1.0 / math.sqrt(HEAD_WIDTH)
    piece = lax.all_gather(local_query, "ctx", axis=0, tiled=True)
    piece_rows = piece.shape[0]
    grouped = piece.reshape(piece_rows, kv_heads, query_group_width, HEAD_WIDTH)
    scores = (
        jnp.einsum("qhgd,khd->qhgk", grouped, key_rows, preferred_element_type=jnp.float32)
        * score_scale
    )
    row_index = jnp.arange(piece_rows, dtype=jnp.int32)
    query_pos = (
        stretch_first + block_order[row_index // half_rows] * half_rows + row_index % half_rows
    )
    allowed = usable[None, :] & (key_pos[None, :] <= query_pos[:, None])
    scores = jnp.where(allowed[:, None, None, :], scores, NEG_FILL)
    stretch_rows = scores.shape[0]
    peaks = lax.pmax(jnp.max(scores, axis=-1), "ctx")
    block_len = math.gcd(stretch_rows, 512)
    block_count = stretch_rows // block_len
    score_blocks = scores.reshape(block_count, block_len, kv_heads, query_group_width, key_count)
    peak_blocks = peaks.reshape(block_count, block_len, kv_heads, query_group_width)

    def weigh_block(inputs):
        block_scores, block_peaks = inputs
        weights = jnp.exp(block_scores - block_peaks[..., None])
        totals = jnp.sum(weights, axis=-1)
        product = jnp.einsum(
            "qhgk,khd->qhgd",
            weights.astype(jnp.bfloat16),
            value_rows,
            preferred_element_type=jnp.float32,
        )
        return (
            product.reshape(block_len, kv_heads * query_group_width * HEAD_WIDTH),
            totals.reshape(block_len, kv_heads * query_group_width),
        )

    sum_blocks, total_blocks = lax.map(weigh_block, (score_blocks, peak_blocks))
    weighted = sum_blocks.reshape(stretch_rows, kv_heads * query_group_width * HEAD_WIDTH)
    totals_all = total_blocks.reshape(stretch_rows, kv_heads * query_group_width)
    part_sums, part_totals = (
        lax.psum_scatter(weighted, "ctx", scatter_dimension=0, tiled=True),
        lax.psum_scatter(totals_all, "ctx", scatter_dimension=0, tiled=True),
    )
    own_rows = part_sums.shape[0]
    result = (
        part_sums.reshape(own_rows, kv_heads * query_group_width, HEAD_WIDTH)
        / part_totals[..., None]
    )
    result = result.reshape(own_rows, kv_heads * query_group_width * HEAD_WIDTH).astype(
        jnp.bfloat16
    )
    return lax.all_to_all(result, "head", split_axis=0, concat_axis=1, tiled=True)


def solution(mesh):
    return jax.shard_map(
        on_device,
        mesh=mesh,
        in_specs=(
            P(("ctx", "head"), None),
            P(("ctx", "head"), None),
            P(("ctx", "head"), None),
            P("ctx", "head"),
            P("ctx", "head"),
            P(),
            P(),
        ),
        out_specs=P(("ctx", "head"), None),
        check_vma=False,
    )
```

profile of v0, /device:TPU:0, one launch (start us, length us, event | category | flops | bytes accessed | tf_op | source)
XLA Modules:
  0.0 212.5 jit_solution(3873993751585935543)
XLA Ops:
  6.5 4.4 %all-to-all-start.1 = ((bf16[2,2,256]{2,0,1:T(2,128)(2,1)}), bf16[2,2,256]{2,0,1:T(2,128)(2,1)S(1)}, u32[]{:S(2)}, u32[]{:S(2)}) async-start(bf16[2,2,256]{2,0,1:T(2,128)(2,1)} %bitcast.60), calls=%async_computation.1 | async-start | bytes 4096 | tf_op jit(solution)/shard_map/all_to_all | solution.py:24
  11.6 0.6 copy-done.1
  12.3 0.6 gather_fusion
  12.9 0.8 gather_fusion.1
  13.7 0.9 copy-done.2
  14.7 3.3 %all-to-all-start = ((bf16[2,2,256]{2,0,1:T(2,128)(2,1)}), bf16[2,2,256]{2,0,1:T(2,128)(2,1)S(1)}, u32[]{:S(2)}, u32[]{:S(2)}) async-start(bf16[2,2,256]{2,0,1:T(2,128)(2,1)} %bitcast), calls=%async_computation | async-start | bytes 4096 | tf_op jit(solution)/shard_map/all_to_all | solution.py:25
  18.1 3.7 %all-to-all-done = bf16[2,2,256]{2,0,1:T(2,128)(2,1)S(1)} async-done(((bf16[2,2,256]{2,0,1:T(2,128)(2,1)}), bf16[2,2,256]{2,0,1:T(2,128)(2,1)S(1)}, u32[]{:S(2)}, u32[]{:S(2)}) %all-to-all-start) | async-done | bytes 2080 | tf_op jit(solution)/shard_map/all_to_all | solution.py:25
  21.8 3.2 %all-to-all-start.2 = ((bf16[2,2,1024]{2,0,1:T(2,128)(2,1)}), bf16[2,2,1024]{2,0,1:T(2,128)(2,1)S(1)}, u32[]{:S(2)}, u32[]{:S(2)}) async-start(bf16[2,2,1024]{2,0,1:T(2,128)(2,1)} %bitcast.11), calls=%async_computation.2 | async-start | bytes 16384 | tf_op jit(solution)/shard_map/all_to_all | solution.py:23
  25.1 0.1 compare_and_fusion
  25.2 0.6 copy-done.3
  25.9 0.6 dynamic-slice.2
  27.1 1.7 all-to-all-done.2
  28.9 22.4 %all-gather = bf16[16,4,1024]{2,1,0:T(4,128)(2,1)S(1)} all-gather(bf16[1,4,1024]{2,1,0:T(4,128)(2,1)S(1)} %reshape.221), channel_id=1, replica_groups=mesh['ctx'=16,'head'=2] {'ctx'}, dimensions={0}, use_global_device_ids=true | all-gather | bytes 139264 | tf_op jit(solution)/shard_map/all_gather | solution.py:50
  51.3 0.4 fusion.19
  51.7 29.8 %pmax.7 = f32[64,2,4]{0,2,1:T(4,128)S(1)} all-reduce(f32[64,2,4]{0,2,1:T(4,128)S(1)} %get-tuple-element.15), channel_id=1, replica_groups=mesh['ctx'=16,'head'=2] {'ctx'}, use_global_device_ids=true, to_apply=%region_1.2 | all-reduce | flops 512 | bytes 4096 | tf_op jit(solution)/shard_map/pmax | solution.py:64
  81.5 0.3 fusion.2
  81.9 29.5 %all-reduce.2 = f32[64,8]{0,1:T(8,128)S(1)} all-reduce(f32[64,8]{0,1:T(8,128)S(1)} %bitcast.57), channel_id=3, replica_groups=mesh['ctx'=16,'head'=2] {'ctx'}, use_global_device_ids=true, to_apply=%region_4.5.clone | all-reduce | flops 512 | bytes 4096
  111.5 0.4 convolution_bitcast_fusion
  111.9 0.2 copy.26
  112.1 0.8 reshape.203
  113.0 84.9 %all-reduce.5.cloned.1.call-done = f32[64,1024]{1,0:T(8,128)} async-done(((f32[64,1024]{1,0:T(8,128)}), f32[64,1024]{1,0:T(8,128)}) %all-reduce.5.cloned.1.call-update) | async-done | bytes 262160
  197.9 0.8 fusion.11
  198.7 6.4 %all_to_all.70 = bf16[2,2,1024]{2,1,0:T(2,128)(2,1)S(1)} all-to-all(bf16[2,2,1024]{2,1,0:T(2,128)(2,1)S(1)} %all_to_all.62), channel_id=1, replica_groups=mesh['ctx'=16,'head'=2] {'head'}, dimensions={0} | all-to-all | bytes 16384 | tf_op jit(solution)/shard_map/all_to_all | solution.py:100
  205.0 0.6 copy.47
  (30 shorter events, 0.7 us)
Async XLA Ops:
  6.5 7.1 %copy-start = (bf16[448,256]{1,0:T(8,128)(2,1)S(1)}, bf16[448,256]{1,0:T(8,128)(2,1)}, u32[]{:S(2)}) copy-start(bf16[448,256]{1,0:T(8,128)(2,1)} %param.10) | copy-start | bytes 688132
  6.5 8.2 %all-to-all-start.1 = ((bf16[2,2,256]{2,0,1:T(2,128)(2,1)}), bf16[2,2,256]{2,0,1:T(2,128)(2,1)S(1)}, u32[]{:S(2)}, u32[]{:S(2)}) async-start(bf16[2,2,256]{2,0,1:T(2,128)(2,1)} %bitcast.60), calls=%async_computation.1 | async-start | bytes 4096 | tf_op jit(solution)/shard_map/all_to_all | solution.py:24
  11.6 0.7 copy-start.1
  13.7 0.9 copy-start.2
  14.7 7.1 %all-to-all-start = ((bf16[2,2,256]{2,0,1:T(2,128)(2,1)}), bf16[2,2,256]{2,0,1:T(2,128)(2,1)S(1)}, u32[]{:S(2)}, u32[]{:S(2)}) async-start(bf16[2,2,256]{2,0,1:T(2,128)(2,1)} %bitcast), calls=%async_computation | async-start | bytes 4096 | tf_op jit(solution)/shard_map/all_to_all | solution.py:25
  21.8 7.0 %all-to-all-start.2 = ((bf16[2,2,1024]{2,0,1:T(2,128)(2,1)}), bf16[2,2,1024]{2,0,1:T(2,128)(2,1)S(1)}, u32[]{:S(2)}, u32[]{:S(2)}) async-start(bf16[2,2,1024]{2,0,1:T(2,128)(2,1)} %bitcast.11), calls=%async_computation.2 | async-start | bytes 16384 | tf_op jit(solution)/shard_map/all_to_all | solution.py:23
  25.1 172.8 %all-reduce.5.cloned.1.call-start = ((), (), s32[]{:S(2)}) async-start(), calls=%async_computation.4 | async-start | bytes 524288
  25.2 0.7 copy-start.3
Sparse Core Ops, SparseCore 0:
  113.0 84.7 all-reduce.4
where the time goes:
time: 213 us; the launch traced here: 212 us
  waiting for transfers between devices  90.3 us (42%)
  blocking collectives  88.1 us (41%)
  between operations  14.8 us (7%)
  starting transfers between devices  10.9 us (5%)
  local copies, waits for them, and re-layouts  6.24 us (3%)
    unnamed x2, waiting for transfers between devices  84.9 us
    pmax x1, blocking collectives, on_device(): peaks = lax.pmax(jnp.max(scores, axis=-1), 'ctx')  29.8 us
    unnamed x1, blocking collectives  29.5 us
    all_gather x1, blocking collectives, on_device(): piece = lax.all_gather(local_query, 'ctx', axis=0, tiled=True)  22.4 us
    all_to_all x1, blocking collectives, on_device(): lax.all_to_all(result, 'head', split_axis=0, concat_axis=1, tiled=True)  6.36 us
    all_to_all x1, starting transfers between devices, on_device(): lax.all_to_all(new_block_keys, 'head', split_axis=1, concat_axis=0, tiled...  4.37 us
  transfers between devices with their start and end apart: 4, of which 3 were waited for; matrix products, arithmetic and copies ran while one was open for 1% of the time, Pallas kernels for 0%

commit v1 on v0

--- a/solution.py
+++ b/solution.py
@@ -47,7 +47,27 @@
         key_count, kv_heads, HEAD_WIDTH
     )
     score_scale = 1.0 / math.sqrt(HEAD_WIDTH)
-    piece = lax.all_gather(local_query, "ctx", axis=0, tiled=True)
+    z2, mid_arr, local_part = (lax.axis_size("ctx"), lax.axis_index("ctx"), local_query.shape[0])
+    grid = tuple(((i0, (i0 + 1) % z2) for i0 in range(z2)))
+    panels = tuple(((i0, (i0 - 1) % z2) for i0 in range(z2)))
+    piece = jnp.zeros(
+        (*local_query.shape[:0], z2 * local_part, *local_query.shape[1:]), local_query.dtype
+    )
+    piece = lax.dynamic_update_slice_in_dim(piece, local_query, mid_arr * local_part, axis=0)
+    value_now = upper = local_query
+    vec_out = z2 // 2
+    m = 1
+    while m < vec_out + 1:
+        value_now = lax.ppermute(value_now, axis_name="ctx", perm=grid)
+        piece = lax.dynamic_update_slice_in_dim(
+            piece, value_now, (mid_arr - m) % z2 * local_part, axis=0
+        )
+        if m < z2 - vec_out:
+            upper = lax.ppermute(upper, axis_name="ctx", perm=panels)
+            piece = lax.dynamic_update_slice_in_dim(
+                piece, upper, (mid_arr + m) % z2 * local_part, axis=0
+            )
+        m += 1
     piece_rows = piece.shape[0]
     grouped = piece.reshape(piece_rows, kv_heads, query_group_width, HEAD_WIDTH)
     scores = (

time: 213 us -> 236 us (1.11)
  starting transfers between devices: 10.9 us -> 41.8 us
  blocking collectives: 88.1 us -> 65.3 us
  waiting for transfers between devices: 90.3 us -> 106 us
    ppermute x0 -> x15, starting transfers between devices: none -> 30.9 us  [the longest x7 30.9 us: on_device(): upper = lax.ppermute(upper, axis_name='ctx', perm=panels)]
    all_gather x1 -> x0, blocking collectives: 22.4 us -> none  [on_device(): piece = lax.all_gather(local_query, 'ctx', axis=0, tiled=True)]
    ppermute x0 -> x15, waiting for transfers between devices: none -> 15 us  [the longest x8 14.8 us: on_device(): value_now = lax.ppermute(value_now, axis_name='ctx', perm=grid)]
  transfers between devices with their start and end apart: 4 -> 19, of which waited for: 3 -> 12; matrix products, arithmetic and copies ran while one was open for 1% -> 1% of each run, Pallas kernels for 0% -> 0%
where the time goes in v1:
time: 236 us
  waiting for transfers between devices  106 us (45%)
  blocking collectives  65.3 us (28%)
  starting transfers between devices  41.8 us (18%)
  between operations  15.1 us (6%)
  local copies, waits for them, and re-layouts  5.11 us (2%)
    unnamed x2, waiting for transfers between devices  84.9 us
    ppermute x7, starting transfers between devices, on_device(): upper = lax.ppermute(upper, axis_name='ctx', perm=panels)  30.9 us
    pmax x1, blocking collectives, on_device(): peaks = lax.pmax(jnp.max(scores, axis=-1), 'ctx')  29.5 us
    unnamed x1, blocking collectives  29.5 us
    ppermute x8, waiting for transfers between devices, on_device(): value_now = lax.ppermute(value_now, axis_name='ctx', perm=grid)  14.8 us
    all_to_all x1, blocking collectives, on_device(): lax.all_to_all(result, 'head', split_axis=0, concat_axis=1, tiled=True)  6.36 us
  transfers between devices with their start and end apart: 19, of which 12 were waited for; matrix products, arithmetic and copies ran while one was open for 1% of the time, Pallas kernels for 0%

profile of v1, /device:TPU:0, one launch (start us, length us, event | category | flops | bytes accessed | tf_op | source)
XLA Modules:
  0.0 235.8 jit_solution(1094296211128028852)
XLA Ops:
  6.5 4.4 %all-to-all-start.1 = ((bf16[2,2,256]{2,0,1:T(2,128)(2,1)}), bf16[2,2,256]{2,0,1:T(2,128)(2,1)S(1)}, u32[]{:S(2)}, u32[]{:S(2)}) async-start(bf16[2,2,256]{2,0,1:T(2,128)(2,1)} %bitcast.60), calls=%async_computation.1 | async-start | bytes 4096 | tf_op jit(solution)/shard_map/all_to_all | solution.py:24
  14.7 3.2 %all-to-all-start = ((bf16[2,2,256]{2,0,1:T(2,128)(2,1)}), bf16[2,2,256]{2,0,1:T(2,128)(2,1)S(1)}, u32[]{:S(2)}, u32[]{:S(2)}) async-start(bf16[2,2,256]{2,0,1:T(2,128)(2,1)} %bitcast), calls=%async_computation | async-start | bytes 4096 | tf_op jit(solution)/shard_map/all_to_all | solution.py:25
  17.9 3.7 %all-to-all-done = bf16[2,2,256]{2,0,1:T(2,128)(2,1)S(1)} async-done(((bf16[2,2,256]{2,0,1:T(2,128)(2,1)}), bf16[2,2,256]{2,0,1:T(2,128)(2,1)S(1)}, u32[]{:S(2)}, u32[]{:S(2)}) %all-to-all-start) | async-done | bytes 2080 | tf_op jit(solution)/shard_map/all_to_all | solution.py:25
  21.7 3.2 %all-to-all-start.2 = ((bf16[2,2,1024]{2,0,1:T(2,128)(2,1)}), bf16[2,2,1024]{2,0,1:T(2,128)(2,1)S(1)}, u32[]{:S(2)}, u32[]{:S(2)}) async-start(bf16[2,2,1024]{2,0,1:T(2,128)(2,1)} %bitcast.11), calls=%async_computation.2 | async-start | bytes 16384 | tf_op jit(solution)/shard_map/all_to_all | solution.py:23
  27.0 1.7 all-to-all-done.2
  28.7 4.4 %collective-permute-start.1 = (bf16[4,1024]{1,0:T(4,128)(2,1)S(1)}, bf16[4,1024]{1,0:T(4,128)(2,1)S(1)}, u32[]{:S(2)}, u32[]{:S(2)}) collective-permute-start(bf16[4,1024]{1,0:T(4,128)(2,1)S(1)} %all_to_all.61), channel_id=1, source_target_pairs={{0,30},{2,0},{4,2},{6,4},{8,6},{10,8},{12,10},{14,12},{16,14},{18,... | collective-permute-start | bytes 24584 | tf_op jit(solution)/shard_map/ppermute | solution.py:66
  33.2 1.3 collective-permute-done
  34.5 4.4 %collective-permute-start.3 = (bf16[4,1024]{1,0:T(4,128)(2,1)S(1)}, bf16[4,1024]{1,0:T(4,128)(2,1)S(1)}, u32[]{:S(2)}, u32[]{:S(2)}) collective-permute-start(bf16[4,1024]{1,0:T(4,128)(2,1)S(1)} %collective-permute-done.1), channel_id=1, source_target_pairs={{0,30},{2,0},{4,2},{6,4},{8,6},{10,8},{12,10},{14,12},{16,14},{18,... | collective-permute-start | bytes 24584 | tf_op jit(solution)/shard_map/ppermute | solution.py:66
  39.0 1.3 collective-permute-done.2
  40.3 4.4 %collective-permute-start.5 = (bf16[4,1024]{1,0:T(4,128)(2,1)S(1)}, bf16[4,1024]{1,0:T(4,128)(2,1)S(1)}, u32[]{:S(2)}, u32[]{:S(2)}) collective-permute-start(bf16[4,1024]{1,0:T(4,128)(2,1)S(1)} %collective-permute-done.3), channel_id=1, source_target_pairs={{0,30},{2,0},{4,2},{6,4},{8,6},{10,8},{12,10},{14,12},{16,14},{18,... | collective-permute-start | bytes 24584 | tf_op jit(solution)/shard_map/ppermute | solution.py:66
  44.7 1.3 collective-permute-done.4
  46.1 4.4 %collective-permute-start.7 = (bf16[4,1024]{1,0:T(4,128)(2,1)S(1)}, bf16[4,1024]{1,0:T(4,128)(2,1)S(1)}, u32[]{:S(2)}, u32[]{:S(2)}) collective-permute-start(bf16[4,1024]{1,0:T(4,128)(2,1)S(1)} %collective-permute-done.5), channel_id=1, source_target_pairs={{0,30},{2,0},{4,2},{6,4},{8,6},{10,8},{12,10},{14,12},{16,14},{18,... | collective-permute-start | bytes 24584 | tf_op jit(solution)/shard_map/ppermute | solution.py:66
  50.5 1.3 collective-permute-done.6
  51.9 4.4 %collective-permute-start.9 = (bf16[4,1024]{1,0:T(4,128)(2,1)S(1)}, bf16[4,1024]{1,0:T(4,128)(2,1)S(1)}, u32[]{:S(2)}, u32[]{:S(2)}) collective-permute-start(bf16[4,1024]{1,0:T(4,128)(2,1)S(1)} %collective-permute-done.7), channel_id=1, source_target_pairs={{0,30},{2,0},{4,2},{6,4},{8,6},{10,8},{12,10},{14,12},{16,14},{18,... | collective-permute-start | bytes 24584 | tf_op jit(solution)/shard_map/ppermute | solution.py:66
  56.3 1.3 collective-permute-done.8
  57.6 4.4 %collective-permute-start.11 = (bf16[4,1024]{1,0:T(4,128)(2,1)S(1)}, bf16[4,1024]{1,0:T(4,128)(2,1)S(1)}, u32[]{:S(2)}, u32[]{:S(2)}) collective-permute-start(bf16[4,1024]{1,0:T(4,128)(2,1)S(1)} %collective-permute-done.9), channel_id=1, source_target_pairs={{0,30},{2,0},{4,2},{6,4},{8,6},{10,8},{12,10},{14,12},{16,14},{18,... | collective-permute-start | bytes 24584 | tf_op jit(solution)/shard_map/ppermute | solution.py:66
  62.1 1.3 collective-permute-done.10
  63.4 4.4 %collective-permute-start.13 = (bf16[4,1024]{1,0:T(4,128)(2,1)S(1)}, bf16[4,1024]{1,0:T(4,128)(2,1)S(1)}, u32[]{:S(2)}, u32[]{:S(2)}) collective-permute-start(bf16[4,1024]{1,0:T(4,128)(2,1)S(1)} %collective-permute-done.11), channel_id=1, source_target_pairs={{0,30},{2,0},{4,2},{6,4},{8,6},{10,8},{12,10},{14,12},{16,14},{18,... | collective-permute-start | bytes 24584 | tf_op jit(solution)/shard_map/ppermute | solution.py:66
  67.8 1.3 collective-permute-done.12
  69.2 5.7 %collective-permute-done.14 = bf16[4,1024]{1,0:T(4,128)(2,1)S(1)} collective-permute-done((bf16[4,1024]{1,0:T(4,128)(2,1)S(1)}, bf16[4,1024]{1,0:T(4,128)(2,1)S(1)}, u32[]{:S(2)}, u32[]{:S(2)}) %collective-permute-start.14) | collective-permute-done | bytes 8224 | tf_op jit(solution)/shard_map/ppermute | solution.py:61
  75.4 29.5 %pmax.7 = f32[64,2,4]{0,2,1:T(4,128)S(1)} all-reduce(f32[64,2,4]{0,2,1:T(4,128)S(1)} %get-tuple-element.15), channel_id=1, replica_groups=mesh['ctx'=16,'head'=2] {'ctx'}, use_global_device_ids=true, to_apply=%region_1.2 | all-reduce | flops 512 | bytes 4096 | tf_op jit(solution)/shard_map/pmax | solution.py:84
  105.2 29.5 %all-reduce.2 = f32[64,8]{0,1:T(8,128)S(1)} all-reduce(f32[64,8]{0,1:T(8,128)S(1)} %bitcast.57), channel_id=3, replica_groups=mesh['ctx'=16,'head'=2] {'ctx'}, use_global_device_ids=true, to_apply=%region_4.5.clone | all-reduce | flops 512 | bytes 4096
  136.3 84.8 %all-reduce.5.cloned.1.call-done = f32[64,1024]{1,0:T(8,128)} async-done(((f32[64,1024]{1,0:T(8,128)}), f32[64,1024]{1,0:T(8,128)}) %all-reduce.5.cloned.1.call-update) | async-done | bytes 262160
  222.0 6.4 %all_to_all.70 = bf16[2,2,1024]{2,1,0:T(2,128)(2,1)S(1)} all-to-all(bf16[2,2,1024]{2,1,0:T(2,128)(2,1)S(1)} %all_to_all.62), channel_id=1, replica_groups=mesh['ctx'=16,'head'=2] {'head'}, dimensions={0} | all-to-all | bytes 16384 | tf_op jit(solution)/shard_map/all_to_all | solution.py:120
  (76 shorter events, 8.6 us)
Async XLA Ops:
  6.5 4.4 %copy-start = (bf16[448,256]{1,0:T(8,128)(2,1)S(1)}, bf16[448,256]{1,0:T(8,128)(2,1)}, u32[]{:S(2)}) copy-start(bf16[448,256]{1,0:T(8,128)(2,1)} %param.10) | copy-start | bytes 688132
  6.5 8.1 %all-to-all-start.1 = ((bf16[2,2,256]{2,0,1:T(2,128)(2,1)}), bf16[2,2,256]{2,0,1:T(2,128)(2,1)S(1)}, u32[]{:S(2)}, u32[]{:S(2)}) async-start(bf16[2,2,256]{2,0,1:T(2,128)(2,1)} %bitcast.60), calls=%async_computation.1 | async-start | bytes 4096 | tf_op jit(solution)/shard_map/all_to_all | solution.py:24
  11.0 0.7 copy-start.1
  12.3 0.9 copy-start.2
  14.7 7.0 %all-to-all-start = ((bf16[2,2,256]{2,0,1:T(2,128)(2,1)}), bf16[2,2,256]{2,0,1:T(2,128)(2,1)S(1)}, u32[]{:S(2)}, u32[]{:S(2)}) async-start(bf16[2,2,256]{2,0,1:T(2,128)(2,1)} %bitcast), calls=%async_computation | async-start | bytes 4096 | tf_op jit(solution)/shard_map/all_to_all | solution.py:25
  21.7 7.0 %all-to-all-start.2 = ((bf16[2,2,1024]{2,0,1:T(2,128)(2,1)}), bf16[2,2,1024]{2,0,1:T(2,128)(2,1)S(1)}, u32[]{:S(2)}, u32[]{:S(2)}) async-start(bf16[2,2,1024]{2,0,1:T(2,128)(2,1)} %bitcast.11), calls=%async_computation.2 | async-start | bytes 16384 | tf_op jit(solution)/shard_map/all_to_all | solution.py:23
  24.9 196.3 %all-reduce.5.cloned.1.call-start = ((), (), s32[]{:S(2)}) async-start(), calls=%async_computation.4 | async-start | bytes 524288
  25.1 0.7 copy-start.3
  28.7 5.8 %collective-permute-start = (bf16[4,1024]{1,0:T(4,128)(2,1)S(1)}, bf16[4,1024]{1,0:T(4,128)(2,1)S(1)}, u32[]{:S(2)}, u32[]{:S(2)}) collective-permute-start(bf16[4,1024]{1,0:T(4,128)(2,1)S(1)} %all_to_all.61), channel_id=1, source_target_pairs={{0,2},{2,4},{4,6},{6,8},{8,10},{10,12},{12,14},{14,16},{16,18},{18... | collective-permute-start | bytes 24584 | tf_op jit(solution)/shard_map/ppermute | solution.py:61
  28.7 5.8 %collective-permute-start.1 = (bf16[4,1024]{1,0:T(4,128)(2,1)S(1)}, bf16[4,1024]{1,0:T(4,128)(2,1)S(1)}, u32[]{:S(2)}, u32[]{:S(2)}) collective-permute-start(bf16[4,1024]{1,0:T(4,128)(2,1)S(1)} %all_to_all.61), channel_id=1, source_target_pairs={{0,30},{2,0},{4,2},{6,4},{8,6},{10,8},{12,10},{14,12},{16,14},{18,... | collective-permute-start | bytes 24584 | tf_op jit(solution)/shard_map/ppermute | solution.py:66
  34.5 5.8 %collective-permute-start.2 = (bf16[4,1024]{1,0:T(4,128)(2,1)S(1)}, bf16[4,1024]{1,0:T(4,128)(2,1)S(1)}, u32[]{:S(2)}, u32[]{:S(2)}) collective-permute-start(bf16[4,1024]{1,0:T(4,128)(2,1)S(1)} %collective-permute-done), channel_id=1, source_target_pairs={{0,2},{2,4},{4,6},{6,8},{8,10},{10,12},{12,14},{14,16},{16,18},{18... | collective-permute-start | bytes 24584 | tf_op jit(solution)/shard_map/ppermute | solution.py:61
  34.5 5.8 %collective-permute-start.3 = (bf16[4,1024]{1,0:T(4,128)(2,1)S(1)}, bf16[4,1024]{1,0:T(4,128)(2,1)S(1)}, u32[]{:S(2)}, u32[]{:S(2)}) collective-permute-start(bf16[4,1024]{1,0:T(4,128)(2,1)S(1)} %collective-permute-done.1), channel_id=1, source_target_pairs={{0,30},{2,0},{4,2},{6,4},{8,6},{10,8},{12,10},{14,12},{16,14},{18,... | collective-permute-start | bytes 24584 | tf_op jit(solution)/shard_map/ppermute | solution.py:66
  40.3 5.8 %collective-permute-start.4 = (bf16[4,1024]{1,0:T(4,128)(2,1)S(1)}, bf16[4,1024]{1,0:T(4,128)(2,1)S(1)}, u32[]{:S(2)}, u32[]{:S(2)}) collective-permute-start(bf16[4,1024]{1,0:T(4,128)(2,1)S(1)} %collective-permute-done.2), channel_id=1, source_target_pairs={{0,2},{2,4},{4,6},{6,8},{8,10},{10,12},{12,14},{14,16},{16,18},{18... | collective-permute-start | bytes 24584 | tf_op jit(solution)/shard_map/ppermute | solution.py:61
  40.3 5.8 %collective-permute-start.5 = (bf16[4,1024]{1,0:T(4,128)(2,1)S(1)}, bf16[4,1024]{1,0:T(4,128)(2,1)S(1)}, u32[]{:S(2)}, u32[]{:S(2)}) collective-permute-start(bf16[4,1024]{1,0:T(4,128)(2,1)S(1)} %collective-permute-done.3), channel_id=1, source_target_pairs={{0,30},{2,0},{4,2},{6,4},{8,6},{10,8},{12,10},{14,12},{16,14},{18,... | collective-permute-start | bytes 24584 | tf_op jit(solution)/shard_map/ppermute | solution.py:66
  46.0 5.8 %collective-permute-start.6 = (bf16[4,1024]{1,0:T(4,128)(2,1)S(1)}, bf16[4,1024]{1,0:T(4,128)(2,1)S(1)}, u32[]{:S(2)}, u32[]{:S(2)}) collective-permute-start(bf16[4,1024]{1,0:T(4,128)(2,1)S(1)} %collective-permute-done.4), channel_id=1, source_target_pairs={{0,2},{2,4},{4,6},{6,8},{8,10},{10,12},{12,14},{14,16},{16,18},{18... | collective-permute-start | bytes 24584 | tf_op jit(solution)/shard_map/ppermute | solution.py:61
  46.1 5.8 %collective-permute-start.7 = (bf16[4,1024]{1,0:T(4,128)(2,1)S(1)}, bf16[4,1024]{1,0:T(4,128)(2,1)S(1)}, u32[]{:S(2)}, u32[]{:S(2)}) collective-permute-start(bf16[4,1024]{1,0:T(4,128)(2,1)S(1)} %collective-permute-done.5), channel_id=1, source_target_pairs={{0,30},{2,0},{4,2},{6,4},{8,6},{10,8},{12,10},{14,12},{16,14},{18,... | collective-permute-start | bytes 24584 | tf_op jit(solution)/shard_map/ppermute | solution.py:66
  51.8 5.8 %collective-permute-start.8 = (bf16[4,1024]{1,0:T(4,128)(2,1)S(1)}, bf16[4,1024]{1,0:T(4,128)(2,1)S(1)}, u32[]{:S(2)}, u32[]{:S(2)}) collective-permute-start(bf16[4,1024]{1,0:T(4,128)(2,1)S(1)} %collective-permute-done.6), channel_id=1, source_target_pairs={{0,2},{2,4},{4,6},{6,8},{8,10},{10,12},{12,14},{14,16},{16,18},{18... | collective-permute-start | bytes 24584 | tf_op jit(solution)/shard_map/ppermute | solution.py:61
  51.9 5.8 %collective-permute-start.9 = (bf16[4,1024]{1,0:T(4,128)(2,1)S(1)}, bf16[4,1024]{1,0:T(4,128)(2,1)S(1)}, u32[]{:S(2)}, u32[]{:S(2)}) collective-permute-start(bf16[4,1024]{1,0:T(4,128)(2,1)S(1)} %collective-permute-done.7), channel_id=1, source_target_pairs={{0,30},{2,0},{4,2},{6,4},{8,6},{10,8},{12,10},{14,12},{16,14},{18,... | collective-permute-start | bytes 24584 | tf_op jit(solution)/shard_map/ppermute | solution.py:66
  57.6 5.8 %collective-permute-start.10 = (bf16[4,1024]{1,0:T(4,128)(2,1)S(1)}, bf16[4,1024]{1,0:T(4,128)(2,1)S(1)}, u32[]{:S(2)}, u32[]{:S(2)}) collective-permute-start(bf16[4,1024]{1,0:T(4,128)(2,1)S(1)} %collective-permute-done.8), channel_id=1, source_target_pairs={{0,2},{2,4},{4,6},{6,8},{8,10},{10,12},{12,14},{14,16},{16,18},{18... | collective-permute-start | bytes 24584 | tf_op jit(solution)/shard_map/ppermute | solution.py:61
  57.6 5.8 %collective-permute-start.11 = (bf16[4,1024]{1,0:T(4,128)(2,1)S(1)}, bf16[4,1024]{1,0:T(4,128)(2,1)S(1)}, u32[]{:S(2)}, u32[]{:S(2)}) collective-permute-start(bf16[4,1024]{1,0:T(4,128)(2,1)S(1)} %collective-permute-done.9), channel_id=1, source_target_pairs={{0,30},{2,0},{4,2},{6,4},{8,6},{10,8},{12,10},{14,12},{16,14},{18,... | collective-permute-start | bytes 24584 | tf_op jit(solution)/shard_map/ppermute | solution.py:66
  63.4 5.8 %collective-permute-start.12 = (bf16[4,1024]{1,0:T(4,128)(2,1)S(1)}, bf16[4,1024]{1,0:T(4,128)(2,1)S(1)}, u32[]{:S(2)}, u32[]{:S(2)}) collective-permute-start(bf16[4,1024]{1,0:T(4,128)(2,1)S(1)} %collective-permute-done.10), channel_id=1, source_target_pairs={{0,2},{2,4},{4,6},{6,8},{8,10},{10,12},{12,14},{14,16},{16,18},{18... | collective-permute-start | bytes 24584 | tf_op jit(solution)/shard_map/ppermute | solution.py:61
  63.4 5.8 %collective-permute-start.13 = (bf16[4,1024]{1,0:T(4,128)(2,1)S(1)}, bf16[4,1024]{1,0:T(4,128)(2,1)S(1)}, u32[]{:S(2)}, u32[]{:S(2)}) collective-permute-start(bf16[4,1024]{1,0:T(4,128)(2,1)S(1)} %collective-permute-done.11), channel_id=1, source_target_pairs={{0,30},{2,0},{4,2},{6,4},{8,6},{10,8},{12,10},{14,12},{16,14},{18,... | collective-permute-start | bytes 24584 | tf_op jit(solution)/shard_map/ppermute | solution.py:66
  69.1 5.8 %collective-permute-start.14 = (bf16[4,1024]{1,0:T(4,128)(2,1)S(1)}, bf16[4,1024]{1,0:T(4,128)(2,1)S(1)}, u32[]{:S(2)}, u32[]{:S(2)}) collective-permute-start(bf16[4,1024]{1,0:T(4,128)(2,1)S(1)} %collective-permute-done.12), channel_id=1, source_target_pairs={{0,2},{2,4},{4,6},{6,8},{8,10},{10,12},{12,14},{14,16},{16,18},{18... | collective-permute-start | bytes 24584 | tf_op jit(solution)/shard_map/ppermute | solution.py:61
Sparse Core Ops, SparseCore 0:
  136.4 84.7 all-reduce.4
